TPU v7x, 256 devices: a whole 4x4x8 slice. The times are simulated.
256 devices in a mesh: seq: 128 (over z, y, x), head: 2 (over core).
Axes of the slice: x: 4, y: 4, z: 8, core: 2. Of those that a mesh axis runs over, the one named last changes fastest.
Arguments:
- input_rows: bfloat16 [32768, 4096], P(('seq', 'head')), may hold values from -40 to 40
- doc_lengths: int32 [64], replicated, may hold values from 1 to 1024, 32768 in all
- w_query: bfloat16 [4096, 4096], P(None, 'head'), may hold values from -0.09375 to 0.09375
- key_weight: bfloat16 [4096, 1024], P(None, 'head'), may hold values from -0.09375 to 0.09375
- value_weight: bfloat16 [4096, 1024], P(None, 'head'), may hold values from -0.09375 to 0.09375
- w_out: bfloat16 [4096, 4096], P('head'), may hold values from -0.5 to 0.5
Outputs:
- mixed: bfloat16 [32768, 4096], P(('seq', 'head'))
All inputs are finite; a program needn't handle non-finite values.
Results may differ from a plain program's by a relative error of at most 0.013.
Values may be sent and summed in bfloat16 or wider, within the bound.
A program may use at most 192 MiB of HBM per device.

v0:
```python
import math
import jax
import jax.numpy as jnp
from jax import lax
from jax.sharding import PartitionSpec as P

HEAD_SIZE = 128
REACH = 4
NEG_FILL = -1e30


def passed_along(value, axis, steps):
    count = lax.axis_size(axis)
    first, last = (max(0, -steps), min(count, count - steps))
    return lax.ppermute(value, axis, [(source, source + steps) for source in range(first, last)])


def inverse_frequency():
    table = []
    for number in range(HEAD_SIZE // 2):
        base_freq = 500000.0 ** (-(2.0 * number) / HEAD_SIZE)
        wavelength = 2.0 * math.pi / base_freq
        smooth = (8192.0 / wavelength - 1.0) / 3.0
        if wavelength < 2048.0:
            table.append(base_freq)
        elif wavelength > 8192.0:
            table.append(base_freq / 8.0)
        else:
            table.append((1.0 - smooth) * base_freq / 8.0 + smooth * base_freq)
    return jnp.asarray(table, dtype=jnp.float32)


def rotate(value_matrix, cosine, sine_table):
    half_size = value_matrix.shape[-1] // 2
    first = value_matrix[..., :half_size]
    second = value_matrix[..., half_size:]
    return jnp.concatenate(
        [first * cosine - second * sine_table, second * cosine + first * sine_table], axis=-1
    )


def doc_of(positions, doc_ends):
    return jnp.sum((positions[:, None] >= doc_ends[None, :]).astype(jnp.int32), axis=1)


def body(input_rows, doc_lengths, w_query, key_weight, value_weight, w_out):
    width_q = w_query.shape[1]
    width_k = key_weight.shape[1]
    heads_here = width_q // HEAD_SIZE
    kv_here = width_k // HEAD_SIZE
    query_group = heads_here // kv_here
    piece = lax.all_gather(input_rows, "head", axis=0, tiled=True)
    projected = jnp.concatenate(
        [
            jnp.dot(piece, w_query, preferred_element_type=jnp.float32),
            jnp.dot(piece, key_weight, preferred_element_type=jnp.float32),
            jnp.dot(piece, value_weight, preferred_element_type=jnp.float32),
        ],
        axis=1,
    )
    tok_seq = projected.shape[0]
    seq_index = lax.axis_index("seq")
    positions = seq_index * tok_seq + jnp.arange(tok_seq, dtype=jnp.int32)
    doc_ends = jnp.cumsum(doc_lengths)
    query_docs = doc_of(positions, doc_ends)
    angles = positions.astype(jnp.float32)[:, None] * inverse_frequency()[None, :]
    cosine = jnp.cos(angles)[:, None, :]
    sine_table = jnp.sin(angles)[:, None, :]
    query_matrix = rotate(
        projected[:, :width_q].reshape(tok_seq, heads_here, HEAD_SIZE), cosine, sine_table
    )
    query_matrix = query_matrix.astype(jnp.bfloat16).reshape(
        tok_seq, kv_here, query_group, HEAD_SIZE
    )
    key_matrix = rotate(
        projected[:, width_q : width_q + width_k].reshape(tok_seq, kv_here, HEAD_SIZE),
        cosine,
        sine_table,
    )
    key_matrix = key_matrix.astype(jnp.bfloat16).reshape(tok_seq, width_k)
    value_matrix = projected[:, width_q + width_k :].astype(jnp.bfloat16)
    scale = HEAD_SIZE ** (-0.5)

    def attend(state, key_rows, value_rows, key_pos):
        running_max, running_sum, weighted = state
        count = key_rows.shape[0]
        key_block = key_rows.reshape(count, kv_here, HEAD_SIZE)
        value_block = value_rows.reshape(count, kv_here, HEAD_SIZE)
        key_docs = doc_of(key_pos, doc_ends)
        scores = (
            jnp.einsum(
                "tkgd,skd->kgts", query_matrix, key_block, preferred_element_type=jnp.float32
            )
            * scale
        )
        allowed = (
            (query_docs[:, None] == key_docs[None, :])
            & (key_pos[None, :] <= positions[:, None])
            & (key_pos[None, :] >= 0)
        )
        scores = jnp.where(allowed, scores, NEG_FILL)
        new_max = jnp.maximum(running_max, jnp.max(scores, axis=-1))
        factor = jnp.exp(running_max - new_max)
        weights = jnp.where(allowed, jnp.exp(scores - new_max[..., None]), 0.0)
        running_sum = running_sum * factor + jnp.sum(weights, axis=-1)
        weighted = weighted * factor[..., None] + jnp.einsum(
            "kgts,skd->kgtd",
            weights.astype(jnp.bfloat16),
            value_block,
            preferred_element_type=jnp.float32,
        )
        return (new_max, running_sum, weighted)

    initial = (
        jnp.full((kv_here, query_group, tok_seq), NEG_FILL, jnp.float32),
        jnp.zeros((kv_here, query_group, tok_seq), jnp.float32),
        jnp.zeros((kv_here, query_group, tok_seq, HEAD_SIZE), jnp.float32),
    )
    state = attend(initial, key_matrix, value_matrix, positions)
    for distance in range(1, REACH + 1):
        earlier = passed_along((key_matrix, value_matrix), "seq", distance)
        state = attend(state, earlier[0], earlier[1], positions - distance * tok_seq)
    final_max, final_sum, final_weighted = state
    attended = (final_weighted / final_sum[..., None]).transpose(2, 0, 1, 3)
    attended = attended.reshape(tok_seq, heads_here * HEAD_SIZE).astype(jnp.bfloat16)
    return lax.psum_scatter(
        jnp.dot(attended, w_out, preferred_element_type=jnp.float32).astype(jnp.bfloat16),
        "head",
        scatter_dimension=0,
        tiled=True,
    )


def solution(mesh):
    in_specs = (
        P(("seq", "head"), None),
        P(),
        P(None, "head"),
        P(None, "head"),
        P(None, "head"),
        P("head", None),
    )
    out_specs = P(("seq", "head"), None)
    return jax.shard_map(body, mesh=mesh, in_specs=in_specs, out_specs=out_specs, check_vma=False)
```

profile of v0, /device:TPU:1, one launch (start us, length us, event | category | flops | bytes accessed | tf_op | source)
XLA Modules:
  0.0 153.8 jit_solution(9673739192024044991)
XLA Ops:
  6.5 0.0 all-gather.2.cloned.1.call-start
  6.5 0.7 all-gather.2.cloned.1.call-update
  7.3 0.0 reduce-scatter.2.cloned.1.call-start
  7.3 0.7 copy.43
  8.1 0.1 reduce-window.8
  8.1 0.1 reduce
  8.3 0.1 convert_reduce_fusion
  8.5 1.2 multiply_cosine_fusion
  9.7 0.7 and_and_fusion.4
  10.4 19.2 %all-gather.2.cloned.1.call-done = bf16[256,4096]{1,0:T(8,128)(2,1)} async-done(((bf16[128,4096]{1,0:T(8,128)(2,1)}), bf16[256,4096]{1,0:T(8,128)(2,1)}) %all-gather.2.cloned.1.call-update) | async-done | bytes 2097168 | tf_op jit(solution)/shard_map/all_gather | solution.py:52
  29.6 4.1 %fusion.94 = f32[256,512]{1,0:T(8,128)S(1)} fusion(bf16[256,4096]{1,0:T(8,128)(2,1)} %all-gather.2.cloned.1.call-done, bf16[4096,512]{1,0:T(8,128)(2,1)} %param.10), kind=kOutput, calls=%fused_computation.140 | convolution fusion | flops 1073741824 | bytes 6815744 | tf_op jit(solution)/shard_map/dot_general | solution.py:56
  33.7 0.2 reshape.280
  33.9 0.3 fusion.93
  34.2 0.1 multiply_subtract_fusion
  34.4 0.1 maximum_convert_fusion
  34.5 0.1 copy.50
  34.7 4.4 %collective-permute-start.2 = (bf16[256,512]{0,1:T(8,128)(2,1)S(1)}, bf16[256,512]{0,1:T(8,128)(2,1)S(1)}, u32[]{:S(2)}, u32[]{:S(2)}) collective-permute-start(bf16[256,512]{0,1:T(8,128)(2,1)S(1)} %bitcast.274), channel_id=1, source_target_pairs={{0,4},{2,6},{4,8},{6,10},{8,12},{10,14},{12,16},{14,18},{16,20},{1... | collective-permute-start | bytes 786440 | tf_op jit(solution)/shard_map/ppermute | solution.py:15
  39.0 2.2 %collective-permute-start = (bf16[256,512]{0,1:T(8,128)(2,1)S(1)}, bf16[256,512]{0,1:T(8,128)(2,1)S(1)}, u32[]{:S(2)}, u32[]{:S(2)}) collective-permute-start(bf16[256,512]{0,1:T(8,128)(2,1)S(1)} %bitcast.275), channel_id=1, source_target_pairs={{0,2},{2,4},{4,6},{6,8},{8,10},{10,12},{12,14},{14,16},{16,18},{18... | collective-permute-start | bytes 786440 | tf_op jit(solution)/shard_map/ppermute | solution.py:15
  41.3 3.1 %collective-permute-start.6 = (bf16[256,512]{0,1:T(8,128)(2,1)S(1)}, bf16[256,512]{0,1:T(8,128)(2,1)S(1)}, u32[]{:S(2)}, u32[]{:S(2)}) collective-permute-start(bf16[256,512]{0,1:T(8,128)(2,1)S(1)} %bitcast.276), channel_id=1, source_target_pairs={{0,8},{2,10},{4,12},{6,14},{8,16},{10,18},{12,20},{14,22},{16,24},... | collective-permute-start | bytes 786440 | tf_op jit(solution)/shard_map/ppermute | solution.py:15
  44.4 5.2 %collective-permute-start.4 = (bf16[256,512]{0,1:T(8,128)(2,1)S(1)}, bf16[256,512]{0,1:T(8,128)(2,1)S(1)}, u32[]{:S(2)}, u32[]{:S(2)}) collective-permute-start(bf16[256,512]{0,1:T(8,128)(2,1)S(1)} %bitcast.277), channel_id=1, source_target_pairs={{0,6},{2,8},{4,10},{6,12},{8,14},{10,16},{12,18},{14,20},{16,22},{... | collective-permute-start | bytes 786440 | tf_op jit(solution)/shard_map/ppermute | solution.py:15
  49.6 4.1 %convolution_convert_fusion.1 = bf16[256,512]{1,0:T(8,128)(2,1)S(1)} fusion(bf16[256,4096]{1,0:T(8,128)(2,1)} %all-gather.2.cloned.1.call-done, bf16[4096,512]{1,0:T(8,128)(2,1)} %param.11), kind=kOutput, calls=%fused_computation.70 | convolution fusion | flops 1073872896 | bytes 6553600 | tf_op jit(solution)/shard_map/dot_general | solution.py:57
  53.7 0.1 copy.78
  53.8 1.3 collective-permute-start.1
  55.1 8.7 %convolution_bitcast_fusion = f32[32,8,16,128]{3,1,2,0:T(8,128)S(1)} fusion(bf16[256,4096]{1,0:T(8,128)(2,1)} %all-gather.2.cloned.1.call-done, bf16[4096,2048]{1,0:T(8,128)(2,1)} %param.9), kind=kOutput, calls=%fused_computation.69 | convolution fusion | flops 4294967296 | bytes 20971520 | tf_op jit(solution)/shard_map/dot_general | solution.py:55
  63.9 0.4 copy.93
  64.3 0.8 subtract_convert_fusion
  65.0 0.3 copy.46
  65.3 0.3 copy.47
  65.6 0.6 pad_maximum_fusion
  66.2 0.8 fusion
  67.0 0.0 collective-permute-done.2
  67.0 4.0 %collective-permute-start.3 = (bf16[256,512]{1,0:T(8,128)(2,1)S(1)}, bf16[256,512]{1,0:T(8,128)(2,1)S(1)}, u32[]{:S(2)}, u32[]{:S(2)}) collective-permute-start(bf16[256,512]{1,0:T(8,128)(2,1)S(1)} %convolution_convert_fusion.1), channel_id=1, source_target_pairs={{0,4},{2,6},{4,8},{6,10},{8,12},{10,14},{12,16},{14,18},{16,20},{1... | collective-permute-start | bytes 786440 | tf_op jit(solution)/shard_map/ppermute | solution.py:15
  71.0 2.9 %fusion.2 = (f32[4,4,256]{2,1,0:T(4,128)S(1)}, f32[4,256,256,4]{2,1,3,0:T(8,128)}) fusion(pred[256,256]{0,1:T(8,128)(4,1)S(1)} %get-tuple-element.28, bf16[256,4,128,1]{0,2,3,1:T(8,128)(2,1)S(1)} %bitcast.272, bf16[256,4,4,128]{3,0,2,1:T(8,128)(2,1)S(1)} %pad_maximum_fusion), kind=kOutput, calls=%fused_computation.13 | convolution fusion | flops 271577088 | bytes 5586944 | tf_op jit(solution)/shard_map/tkgd,skd->kgts/dot_general | solution.py:91
  73.8 0.0 collective-permute-done
  73.8 3.7 %collective-permute-start.5 = (bf16[256,512]{1,0:T(8,128)(2,1)S(1)}, bf16[256,512]{1,0:T(8,128)(2,1)S(1)}, u32[]{:S(2)}, u32[]{:S(2)}) collective-permute-start(bf16[256,512]{1,0:T(8,128)(2,1)S(1)} %convolution_convert_fusion.1), channel_id=1, source_target_pairs={{0,6},{2,8},{4,10},{6,12},{8,14},{10,16},{12,18},{14,20},{16,22},{... | collective-permute-start | bytes 786440 | tf_op jit(solution)/shard_map/ppermute | solution.py:15
  77.6 0.9 fusion.1
  78.5 0.0 collective-permute-done.6
  78.5 3.3 %collective-permute-start.7 = (bf16[256,512]{1,0:T(8,128)(2,1)S(1)}, bf16[256,512]{1,0:T(8,128)(2,1)S(1)}, u32[]{:S(2)}, u32[]{:S(2)}) collective-permute-start(bf16[256,512]{1,0:T(8,128)(2,1)S(1)} %convolution_convert_fusion.1), channel_id=1, source_target_pairs={{0,8},{2,10},{4,12},{6,14},{8,16},{10,18},{12,20},{14,22},{16,24},... | collective-permute-start | bytes 786440 | tf_op jit(solution)/shard_map/ppermute | solution.py:15
  81.8 2.8 %fusion.4 = (f32[4,4,256]{2,1,0:T(4,128)S(1)}, f32[4,256,256,4]{2,1,3,0:T(8,128)}) fusion(pred[256,256]{0,1:T(8,128)(4,1)S(1)} %get-tuple-element.30, bf16[256,4,128,1]{0,2,3,1:T(8,128)(2,1)S(1)} %bitcast.270, bf16[256,4,4,128]{3,0,2,1:T(8,128)(2,1)S(1)} %pad_maximum_fusion), kind=kOutput, calls=%fused_computation.15 | convolution fusion | flops 271577088 | bytes 5586944 | tf_op jit(solution)/shard_map/tkgd,skd->kgts/dot_general | solution.py:91
  84.6 0.0 collective-permute-done.4
  84.6 2.9 %fusion.3 = (f32[4,4,256]{2,1,0:T(4,128)S(1)}, f32[4,256,256,4]{2,1,3,0:T(8,128)}) fusion(pred[256,256]{0,1:T(8,128)(4,1)S(1)} %get-tuple-element.29, bf16[256,4,128,1]{0,2,3,1:T(8,128)(2,1)S(1)} %bitcast.269, bf16[256,4,4,128]{3,0,2,1:T(8,128)(2,1)S(1)} %pad_maximum_fusion), kind=kOutput, calls=%fused_computation.14 | convolution fusion | flops 271577088 | bytes 5586944 | tf_op jit(solution)/shard_map/tkgd,skd->kgts/dot_general | solution.py:91
  87.5 1.0 fusion.5
  88.5 2.5 %fusion.23 = f32[4,4,256,128]{2,3,1,0:T(8,128)} fusion(bf16[256,4,128,1]{0,2,3,1:T(8,128)(2,1)S(1)} %bitcast.273, f32[4,256,256,4]{2,1,3,0:T(8,128)S(1)} %get-tuple-element.43, f32[4,4,256]{2,1,0:T(4,128)S(1)} %get-tuple-element.26, pred[256,256]{0,1:T(8,128)(4,1)S(1)} %get-tuple-element.27), kind=kOutput, calls=%fused_computation.30 | convolution fusion | flops 273678336 | bytes 6635520 | tf_op jit(solution)/shard_map/kgts,skd->kgtd/dot_general | solution.py:106
  91.1 0.0 copy-done.3
  91.1 1.0 fusion.7
  92.1 0.0 collective-permute-done.1
  92.1 0.1 copy.81
  92.3 4.9 %fusion.21 = f32[4,4,256,128]{2,3,1,0:T(8,128)} fusion(bf16[256,4,128,1]{0,2,3,1:T(8,128)(2,1)S(1)} %bitcast.279, f32[4,256,256,4]{2,1,3,0:T(8,128)} %copy-done.3, f32[4,4,256]{2,1,0:T(4,128)S(1)} %get-tuple-element.17, pred[256,256]{0,1:T(8,128)(4,1)S(1)} %get-tuple-element.31), kind=kOutput, calls=%fused_computation.29 | convolution fusion | flops 273678336 | bytes 6635520 | tf_op jit(solution)/shard_map/kgts,skd->kgtd/dot_general | solution.py:106
  97.2 1.0 fusion.9
  98.2 0.0 collective-permute-done.3
  98.2 0.1 copy.84
  98.4 4.9 %fusion.19 = f32[4,4,256,128]{2,3,1,0:T(8,128)} fusion(bf16[256,4,128,1]{0,2,3,1:T(8,128)(2,1)S(1)} %bitcast.280, f32[4,256,256,4]{2,1,3,0:T(8,128)} %get-tuple-element.39, f32[4,4,256]{2,1,0:T(4,128)S(1)} %get-tuple-element.16, pred[256,256]{0,1:T(8,128)(4,1)S(1)} %get-tuple-element.28), kind=kOutput, calls=%fused_computation.28 | convolution fusion | flops 273678336 | bytes 6635520 | tf_op jit(solution)/shard_map/kgts,skd->kgtd/dot_general | solution.py:106
  103.3 0.0 copy-done.2
  103.3 1.0 fusion.11
  104.3 0.0 collective-permute-done.5
  104.3 0.1 copy.87
  104.5 4.9 %fusion.17 = f32[4,4,256,128]{2,3,1,0:T(8,128)} fusion(bf16[256,4,128,1]{0,2,3,1:T(8,128)(2,1)S(1)} %bitcast.281, f32[4,256,256,4]{2,1,3,0:T(8,128)} %get-tuple-element.37, f32[4,4,256]{2,1,0:T(4,128)S(1)} %get-tuple-element.15, pred[256,256]{0,1:T(8,128)(4,1)S(1)} %get-tuple-element.29), kind=kOutput, calls=%fused_computation.27 | convolution fusion | flops 273678336 | bytes 6635520 | tf_op jit(solution)/shard_map/kgts,skd->kgtd/dot_general | solution.py:106
  109.3 1.0 fusion.13
  110.4 0.0 collective-permute-done.7
  110.4 0.1 copy.90
  110.6 6.6 %fusion.26 = bf16[256,4,4,128]{0,3,2,1:T(8,128)(2,1)S(1)} fusion(f32[4,4,256,128]{2,3,1,0:T(8,128)} %fusion.17, f32[4,4,256,128]{2,3,1,0:T(8,128)} %fusion.19, f32[4,4,256,128]{2,3,1,0:T(8,128)} %fusion.21, f32[4,4,256,128]{2,3,1,0:T(8,128)} %fusion.23, f32[256,4,4]{0,2,1:T(4,128)S(1)} %get-tuple-element.10, f32[256,4,4]{0,2,1:T(4,128)S(1)} %get-tuple-element.13, ...), kind=kOutput, calls=%fused_computation.33 | convolution fusion | flops 279445504 | bytes 14073856 | tf_op jit(solution)/shard_map/kgts,skd->kgtd/dot_general | solution.py:106
  117.2 11.6 %convolution_convert_fusion = bf16[256,4096]{1,0:T(8,128)(2,1)} fusion(bf16[256,2048]{0,1:T(8,128)(2,1)S(1)} %bitcast.268, bf16[2048,4096]{1,0:T(8,128)(2,1)} %param.12), kind=kOutput, calls=%fused_computation | convolution fusion | flops 4296015872 | bytes 19922944 | tf_op jit(solution)/shard_map/dot_general | solution.py:127
  128.8 0.0 reduce-scatter.2.cloned.1.call-update
  128.8 18.1 %reduce-scatter.2.cloned.1.call-done = bf16[128,4096]{1,0:T(8,128)(2,1)} async-done(((bf16[256,4096]{1,0:T(8,128)(2,1)}), bf16[128,4096]{1,0:T(8,128)(2,1)}) %reduce-scatter.2.cloned.1.call-update) | async-done | bytes 1048592 | tf_op jit(solution)/shard_map/reduce_scatter | solution.py:126
  (14 shorter events, 0.1 us)
Async XLA Ops:
  6.5 23.1 %all-gather.2.cloned.1.call-start = ((), (), s32[]{:S(2)}) async-start(), calls=%async_computation.1 | async-start | bytes 3145728 | tf_op jit(solution)/shard_map/all_gather | solution.py:52
  7.3 139.7 %reduce-scatter.2.cloned.1.call-start = ((), (), s32[]{:S(2)}) async-start(), calls=%async_computation.2 | async-start | bytes 3145728 | tf_op jit(solution)/shard_map/reduce_scatter | solution.py:126
  34.7 32.3 %collective-permute-start.2 = (bf16[256,512]{0,1:T(8,128)(2,1)S(1)}, bf16[256,512]{0,1:T(8,128)(2,1)S(1)}, u32[]{:S(2)}, u32[]{:S(2)}) collective-permute-start(bf16[256,512]{0,1:T(8,128)(2,1)S(1)} %bitcast.274), channel_id=1, source_target_pairs={{0,4},{2,6},{4,8},{6,10},{8,12},{10,14},{12,16},{14,18},{16,20},{1... | collective-permute-start | bytes 786440 | tf_op jit(solution)/shard_map/ppermute | solution.py:15
  39.0 34.8 %collective-permute-start = (bf16[256,512]{0,1:T(8,128)(2,1)S(1)}, bf16[256,512]{0,1:T(8,128)(2,1)S(1)}, u32[]{:S(2)}, u32[]{:S(2)}) collective-permute-start(bf16[256,512]{0,1:T(8,128)(2,1)S(1)} %bitcast.275), channel_id=1, source_target_pairs={{0,2},{2,4},{4,6},{6,8},{8,10},{10,12},{12,14},{14,16},{16,18},{18... | collective-permute-start | bytes 786440 | tf_op jit(solution)/shard_map/ppermute | solution.py:15
  41.3 37.2 %collective-permute-start.6 = (bf16[256,512]{0,1:T(8,128)(2,1)S(1)}, bf16[256,512]{0,1:T(8,128)(2,1)S(1)}, u32[]{:S(2)}, u32[]{:S(2)}) collective-permute-start(bf16[256,512]{0,1:T(8,128)(2,1)S(1)} %bitcast.276), channel_id=1, source_target_pairs={{0,8},{2,10},{4,12},{6,14},{8,16},{10,18},{12,20},{14,22},{16,24},... | collective-permute-start | bytes 786440 | tf_op jit(solution)/shard_map/ppermute | solution.py:15
  44.4 40.2 %collective-permute-start.4 = (bf16[256,512]{0,1:T(8,128)(2,1)S(1)}, bf16[256,512]{0,1:T(8,128)(2,1)S(1)}, u32[]{:S(2)}, u32[]{:S(2)}) collective-permute-start(bf16[256,512]{0,1:T(8,128)(2,1)S(1)} %bitcast.277), channel_id=1, source_target_pairs={{0,6},{2,8},{4,10},{6,12},{8,14},{10,16},{12,18},{14,20},{16,22},{... | collective-permute-start | bytes 786440 | tf_op jit(solution)/shard_map/ppermute | solution.py:15
  53.8 38.3 %collective-permute-start.1 = (bf16[256,512]{1,0:T(8,128)(2,1)S(1)}, bf16[256,512]{1,0:T(8,128)(2,1)S(1)}, u32[]{:S(2)}, u32[]{:S(2)}) collective-permute-start(bf16[256,512]{1,0:T(8,128)(2,1)S(1)} %convolution_convert_fusion.1), channel_id=1, source_target_pairs={{0,2},{2,4},{4,6},{6,8},{8,10},{10,12},{12,14},{14,16},{16,18},{18... | collective-permute-start | bytes 786440 | tf_op jit(solution)/shard_map/ppermute | solution.py:15
  67.0 31.2 %collective-permute-start.3 = (bf16[256,512]{1,0:T(8,128)(2,1)S(1)}, bf16[256,512]{1,0:T(8,128)(2,1)S(1)}, u32[]{:S(2)}, u32[]{:S(2)}) collective-permute-start(bf16[256,512]{1,0:T(8,128)(2,1)S(1)} %convolution_convert_fusion.1), channel_id=1, source_target_pairs={{0,4},{2,6},{4,8},{6,10},{8,12},{10,14},{12,16},{14,18},{16,20},{1... | collective-permute-start | bytes 786440 | tf_op jit(solution)/shard_map/ppermute | solution.py:15
  73.8 30.5 %collective-permute-start.5 = (bf16[256,512]{1,0:T(8,128)(2,1)S(1)}, bf16[256,512]{1,0:T(8,128)(2,1)S(1)}, u32[]{:S(2)}, u32[]{:S(2)}) collective-permute-start(bf16[256,512]{1,0:T(8,128)(2,1)S(1)} %convolution_convert_fusion.1), channel_id=1, source_target_pairs={{0,6},{2,8},{4,10},{6,12},{8,14},{10,16},{12,18},{14,20},{16,22},{... | collective-permute-start | bytes 786440 | tf_op jit(solution)/shard_map/ppermute | solution.py:15
  78.5 12.6 %copy-start.3 = (f32[4,256,256,4]{2,1,3,0:T(8,128)}, f32[4,256,256,4]{2,1,3,0:T(8,128)S(1)}, u32[]{:S(2)}) copy-start(f32[4,256,256,4]{2,1,3,0:T(8,128)S(1)} %get-tuple-element.41) | copy-start | bytes 12582916
  78.5 31.9 %collective-permute-start.7 = (bf16[256,512]{1,0:T(8,128)(2,1)S(1)}, bf16[256,512]{1,0:T(8,128)(2,1)S(1)}, u32[]{:S(2)}, u32[]{:S(2)}) collective-permute-start(bf16[256,512]{1,0:T(8,128)(2,1)S(1)} %convolution_convert_fusion.1), channel_id=1, source_target_pairs={{0,8},{2,10},{4,12},{6,14},{8,16},{10,18},{12,20},{14,22},{16,24},... | collective-permute-start | bytes 786440 | tf_op jit(solution)/shard_map/ppermute | solution.py:15
  92.3 4.9 %copy-start.1 = (f32[4,256,256,4]{2,1,3,0:T(8,128)S(1)}, f32[4,256,256,4]{2,1,3,0:T(8,128)}, u32[]{:S(2)}) copy-start(f32[4,256,256,4]{2,1,3,0:T(8,128)} %get-tuple-element.39) | copy-start | bytes 12582916
  98.4 4.9 %copy-start.2 = (f32[4,256,256,4]{2,1,3,0:T(8,128)S(1)}, f32[4,256,256,4]{2,1,3,0:T(8,128)}, u32[]{:S(2)}) copy-start(f32[4,256,256,4]{2,1,3,0:T(8,128)} %get-tuple-element.37) | copy-start | bytes 12582916
  104.5 4.9 %copy-start = (f32[4,256,256,4]{2,1,3,0:T(8,128)S(1)}, f32[4,256,256,4]{2,1,3,0:T(8,128)}, u32[]{:S(2)}) copy-start(f32[4,256,256,4]{2,1,3,0:T(8,128)} %get-tuple-element.35) | copy-start | bytes 12582916
Sparse Core Ops, SparseCore 0:
  9.2 20.4 all-gather.1
  128.9 17.9 reduce-scatter.1
where the time goes:
time: 154 us
  matrix products  62.4 us (41%)
  waiting for transfers between devices  38.1 us (25%)
  starting transfers between devices  27.3 us (18%)
  between operations  13.8 us (9%)
  other arithmetic  9.22 us (6%)
  local copies, waits for them, and re-layouts  3.01 us (2%)
    ppermute x8, starting transfers between devices, passed_along(): lax.ppermute(value, axis, [(source, source + steps) for source in range(f...  27.2 us
    dot_general x5, matrix products, attend(): jnp.einsum('kgts,skd->kgtd', weights.astype(jnp.bfloat16), value_block, p...  23.8 us
    all_gather x1, waiting for transfers between devices, body(): piece = lax.all_gather(input_rows, 'head', axis=0, tiled=True)  19.2 us
    reduce_scatter x1, waiting for transfers between devices, body(): lax.psum_scatter(jnp.dot(attended, w_out, preferred_element_type=jnp.floa...  18.1 us
    dot_general x1, matrix products, body(): jnp.dot(attended, w_out, preferred_element_type=jnp.float32)  11.6 us
    dot_general x5, matrix products, attend(): jnp.einsum('tkgd,skd->kgts', query_matrix, key_block, preferred_element_t...  10.2 us
    dot_general x1, matrix products, body(): jnp.dot(piece, w_query, preferred_element_type=jnp.float32)  8.73 us
    reduce_sum x5, other arithmetic, attend(): running_sum = running_sum * factor + jnp.sum(weights, axis=-1)  5.24 us
  transfers between devices with their start and end apart: 10, of which 2 were waited for; matrix products, arithmetic and copies ran while one was open for 33% of the time, Pallas kernels for 0%

commit v1 on v0

--- a/solution.py
+++ b/solution.py
@@ -49,7 +49,9 @@
     heads_here = width_q // HEAD_SIZE
     kv_here = width_k // HEAD_SIZE
     query_group = heads_here // kv_here
-    piece = lax.all_gather(input_rows, "head", axis=0, tiled=True)
+    piece = jnp.concatenate(
+        lax.all_to_all(jnp.stack([input_rows] * lax.axis_size("head")), "head", 0, 0), axis=0
+    )
     projected = jnp.concatenate(
         [
             jnp.dot(piece, w_query, preferred_element_type=jnp.float32),

time: 154 us -> 175 us (1.14)
  local copies, waits for them, and re-layouts: 3.01 us -> 31.5 us
  waiting for transfers between devices: 38.1 us -> 19.1 us
  starting transfers between devices: 27.3 us -> 33.3 us
  other arithmetic: 9.22 us -> 14.2 us
    dot_general x0 -> x2, local copies, waits for them, and re-layouts: none -> 27.2 us  [the longest x1 20.7 us: body(): jnp.dot(piece, w_query, preferred_element_type=jnp.float32)]
    all_gather x1 -> x0, waiting for transfers between devices: 19.2 us -> none  [body(): piece = lax.all_gather(input_rows, 'head', axis=0, tiled=True)]
    all_to_all x0 -> x1, starting transfers between devices: none -> 6.99 us  [body(): lax.all_to_all(jnp.stack([input_rows] * lax.axis_size('head')), 'head', 0...]
    another operation x3 -> x4, other arithmetic: 0.97 us -> 4.12 us  [the longest x1 3.06 us: body(): jnp.stack([input_rows] * lax.axis_size('head'))]
    reshape x5, local copies, waits for them, and re-layouts: 0.66 us -> 3.28 us  [attend(): value_block = value_rows.reshape(count, kv_here, HEAD_SIZE)]
    dot_general x1, matrix products: 4.06 us -> 2.01 us  [body(): jnp.dot(piece, value_weight, preferred_element_type=jnp.float32)]
    dot_general x5, matrix products: 10.2 us -> 12.2 us  [attend(): jnp.einsum('tkgd,skd->kgts', query_matrix, key_block, preferred_element_t...]
  transfers between devices with their start and end apart: 10 -> 10, of which waited for: 2 -> 1; matrix products, arithmetic and copies ran while one was open for 33% -> 47% of each run, Pallas kernels for 0% -> 0%
where the time goes in v1:
time: 175 us; the launch traced here: 173 us
  matrix products  61.3 us (35%)
  starting transfers between devices  33.3 us (19%)
  local copies, waits for them, and re-layouts  31.5 us (18%)
  waiting for transfers between devices  19.1 us (11%)
  other arithmetic  14.2 us (8%)
  between operations  13.8 us (8%)
    ppermute x8, starting transfers between devices, passed_along(): lax.ppermute(value, axis, [(source, source + steps) for source in range(f...  26.3 us
    dot_general x5, matrix products, attend(): jnp.einsum('kgts,skd->kgtd', weights.astype(jnp.bfloat16), value_block, p...  23.8 us
    dot_general x1, local copies, waits for them, and re-layouts, body(): jnp.dot(piece, w_query, preferred_element_type=jnp.float32)  20.7 us
    reduce_scatter x1, waiting for transfers between devices, body(): lax.psum_scatter(jnp.dot(attended, w_out, preferred_element_type=jnp.floa...  19.1 us
    dot_general x5, matrix products, attend(): jnp.einsum('tkgd,skd->kgts', query_matrix, key_block, preferred_element_t...  12.2 us
    dot_general x1, matrix products, body(): jnp.dot(attended, w_out, preferred_element_type=jnp.float32)  11.6 us
    dot_general x1, matrix products, body(): jnp.dot(piece, w_query, preferred_element_type=jnp.float32)  8.16 us
    all_to_all x1, starting transfers between devices, body(): lax.all_to_all(jnp.stack([input_rows] * lax.axis_size('head')), 'head', 0...  6.99 us
  transfers between devices with their start and end apart: 10, of which 1 were waited for; matrix products, arithmetic and copies ran while one was open for 47% of the time, Pallas kernels for 0%

profile of v1, /device:TPU:1, one launch (start us, length us, event | category | flops | bytes accessed | tf_op | source)
XLA Modules:
  0.0 173.4 jit_solution(13545069527181864365)
XLA Ops:
  6.5 3.1 %pad_maximum_fusion = bf16[2,128,4096]{2,1,0:T(8,128)(2,1)} fusion(bf16[1,128,4096]{2,1,0:T(8,128)(2,1)} %bitcast.280), kind=kLoop, calls=%fused_computation.31 | loop fusion | flops 1048576 | bytes 3145728 | tf_op jit(solution)/shard_map/stack | solution.py:53
  9.6 7.0 %all-to-all-start = ((bf16[2,128,4096]{2,1,0:T(8,128)(2,1)}), bf16[2,128,4096]{2,1,0:T(8,128)(2,1)S(1)}, u32[]{:S(2)}, u32[]{:S(2)}) async-start(bf16[2,128,4096]{2,1,0:T(8,128)(2,1)} %pad_maximum_fusion), calls=%async_computation | async-start | bytes 4194304 | tf_op jit(solution)/shard_map/all_to_all | solution.py:53
  16.6 6.4 %copy.79 = bf16[512,4096]{1,0:T(8,128)(2,1)} copy(bf16[512,4096]{0,1:T(8,128)(2,1)} %bitcast.272) | data formatting | bytes 8388608 | tf_op jit(solution)/shard_map/dot_general | solution.py:58
  23.0 0.3 multiply_cosine_fusion
  23.3 0.0 all-to-all-done
  23.3 0.0 copy-start.14
  23.4 3.6 %fusion.93 = f32[256,4,128]{0,2,1:T(8,128)S(1)} fusion(bf16[256,4096,1]{1,0,2:T(8,128)(2,1)S(1)} %bitcast.276, bf16[4,128,4096]{2,1,0:T(8,128)(2,1)} %bitcast.273), kind=kOutput, calls=%fused_computation.139 | convolution fusion | flops 1073741824 | bytes 6815744 | tf_op jit(solution)/shard_map/dot_general | solution.py:58
  27.0 0.1 multiply_subtract_fusion
  27.1 0.7 maximum_convert_fusion
  27.8 2.2 %collective-permute-start = (bf16[256,512]{0,1:T(8,128)(2,1)}, bf16[256,512]{0,1:T(8,128)(2,1)}, u32[]{:S(2)}, u32[]{:S(2)}) collective-permute-start(bf16[256,512]{0,1:T(8,128)(2,1)} %bitcast.18), channel_id=1, source_target_pairs={{0,2},{2,4},{4,6},{6,8},{8,10},{10,12},{12,14},{14,16},{16,18},{18... | collective-permute-start | bytes 786440 | tf_op jit(solution)/shard_map/ppermute | solution.py:15
  30.0 4.4 %collective-permute-start.2 = (bf16[256,512]{0,1:T(8,128)(2,1)}, bf16[256,512]{0,1:T(8,128)(2,1)}, u32[]{:S(2)}, u32[]{:S(2)}) collective-permute-start(bf16[256,512]{0,1:T(8,128)(2,1)} %bitcast.18), channel_id=1, source_target_pairs={{0,4},{2,6},{4,8},{6,10},{8,12},{10,14},{12,16},{14,18},{16,20},{1... | collective-permute-start | bytes 786440 | tf_op jit(solution)/shard_map/ppermute | solution.py:15
  34.4 2.5 %collective-permute-start.6 = (bf16[256,512]{0,1:T(8,128)(2,1)}, bf16[256,512]{0,1:T(8,128)(2,1)S(1)}, u32[]{:S(2)}, u32[]{:S(2)}) collective-permute-start(bf16[256,512]{0,1:T(8,128)(2,1)} %bitcast.18), channel_id=1, source_target_pairs={{0,8},{2,10},{4,12},{6,14},{8,16},{10,18},{12,20},{14,22},{16,24},... | collective-permute-start | bytes 786440 | tf_op jit(solution)/shard_map/ppermute | solution.py:15
  36.9 4.1 %collective-permute-start.4 = (bf16[256,512]{0,1:T(8,128)(2,1)}, bf16[256,512]{0,1:T(8,128)(2,1)S(1)}, u32[]{:S(2)}, u32[]{:S(2)}) collective-permute-start(bf16[256,512]{0,1:T(8,128)(2,1)} %bitcast.18), channel_id=1, source_target_pairs={{0,6},{2,8},{4,10},{6,12},{8,14},{10,16},{12,18},{14,20},{16,22},{... | collective-permute-start | bytes 786440 | tf_op jit(solution)/shard_map/ppermute | solution.py:15
  41.0 2.0 %convolution_convert_fusion.1 = bf16[256,512]{1,0:T(8,128)(2,1)} fusion(bf16[256,4096]{1,0:T(8,128)(2,1)S(1)} %bitcast.277, bf16[4096,512]{1,0:T(8,128)(2,1)S(1)} %copy-done.14), kind=kOutput, calls=%fused_computation.68 | convolution fusion | flops 1073872896 | bytes 6553600 | tf_op jit(solution)/shard_map/dot_general | solution.py:59
  43.0 2.9 %collective-permute-start.1 = (bf16[256,512]{1,0:T(8,128)(2,1)}, bf16[256,512]{1,0:T(8,128)(2,1)}, u32[]{:S(2)}, u32[]{:S(2)}) collective-permute-start(bf16[256,512]{1,0:T(8,128)(2,1)} %convolution_convert_fusion.1), channel_id=1, source_target_pairs={{0,2},{2,4},{4,6},{6,8},{8,10},{10,12},{12,14},{14,16},{16,18},{18... | collective-permute-start | bytes 786440 | tf_op jit(solution)/shard_map/ppermute | solution.py:15
  45.9 0.6 fusion.69
  46.5 0.6 fusion.73
  47.1 0.6 broadcast_compare_fusion.1
  47.7 0.5 broadcast_compare_fusion.3
  48.2 1.8 %copy.83 = bf16[256,512]{0,1:T(8,128)(2,1)} copy(bf16[256,512]{1,0:T(8,128)(2,1)} %convolution_convert_fusion.1) | data formatting | bytes 524288 | tf_op jit(solution)/shard_map/reshape | solution.py:90
  50.0 0.1 copy.44
  50.1 0.1 reduce-window.8
  50.2 0.6 reduce
  50.9 20.7 %copy.82 = bf16[2048,4096]{1,0:T(8,128)(2,1)} copy(bf16[2048,4096]{0,1:T(8,128)(2,1)} %bitcast.270) | data formatting | bytes 33554432 | tf_op jit(solution)/shard_map/dot_general | solution.py:57
  71.6 8.2 %fusion.94 = f32[256,16,128]{0,2,1:T(8,128)S(1)} fusion(bf16[256,4096,1]{1,0,2:T(8,128)(2,1)S(1)} %bitcast.278, bf16[16,128,4096]{2,1,0:T(8,128)(2,1)} %bitcast.271), kind=kOutput, calls=%fused_computation.140 | convolution fusion | flops 4294967296 | bytes 20971520 | tf_op jit(solution)/shard_map/dot_general | solution.py:57
  79.8 0.3 subtract_convert_fusion
  80.2 0.5 copy.47
  80.6 0.5 copy.48
  81.1 0.6 pad_maximum_fusion.1
  81.7 0.1 convert_reduce_fusion
  81.9 0.7 and_and_fusion.4
  82.6 0.9 fusion
  83.6 0.0 collective-permute-done
  83.6 2.4 %collective-permute-start.3 = (bf16[256,512]{1,0:T(8,128)(2,1)}, bf16[256,512]{1,0:T(8,128)(2,1)S(1)}, u32[]{:S(2)}, u32[]{:S(2)}) collective-permute-start(bf16[256,512]{1,0:T(8,128)(2,1)} %convolution_convert_fusion.1), channel_id=1, source_target_pairs={{0,4},{2,6},{4,8},{6,10},{8,12},{10,14},{12,16},{14,18},{16,20},{1... | collective-permute-start | bytes 786440 | tf_op jit(solution)/shard_map/ppermute | solution.py:15
  86.0 1.8 %fusion.1 = (f32[4,4,256]{2,1,0:T(4,128)S(1)}, f32[4,256,256,4]{2,1,3,0:T(8,128)S(1)}) fusion(pred[256,256]{0,1:T(8,128)(4,1)S(1)} %get-tuple-element.29, bf16[256,4,128,1]{0,2,3,1:T(8,128)(2,1)} %bitcast.61, bf16[256,4,4,128]{3,0,2,1:T(8,128)(2,1)S(1)} %pad_maximum_fusion.1), kind=kOutput, calls=%fused_computation.12 | convolution fusion | flops 271577088 | bytes 5586944 | tf_op jit(solution)/shard_map/tkgd,skd->kgts/dot_general | solution.py:93
  87.9 0.0 collective-permute-done.2
  87.9 4.4 %collective-permute-start.5 = (bf16[256,512]{1,0:T(8,128)(2,1)}, bf16[256,512]{1,0:T(8,128)(2,1)S(1)}, u32[]{:S(2)}, u32[]{:S(2)}) collective-permute-start(bf16[256,512]{1,0:T(8,128)(2,1)} %convolution_convert_fusion.1), channel_id=1, source_target_pairs={{0,6},{2,8},{4,10},{6,12},{8,14},{10,16},{12,18},{14,20},{16,22},{... | collective-permute-start | bytes 786440 | tf_op jit(solution)/shard_map/ppermute | solution.py:15
  92.3 3.8 %fusion.2 = (f32[4,4,256]{2,1,0:T(4,128)S(1)}, f32[4,256,256,4]{2,1,3,0:T(8,128)}) fusion(pred[256,256]{0,1:T(8,128)(4,1)S(1)} %get-tuple-element.26, bf16[256,4,128,1]{0,2,3,1:T(8,128)(2,1)} %bitcast.65, bf16[256,4,4,128]{3,0,2,1:T(8,128)(2,1)S(1)} %pad_maximum_fusion.1), kind=kOutput, calls=%fused_computation.13 | convolution fusion | flops 271577088 | bytes 5586944 | tf_op jit(solution)/shard_map/tkgd,skd->kgts/dot_general | solution.py:93
  96.1 0.0 collective-permute-done.6
  96.1 3.4 %collective-permute-start.7 = (bf16[256,512]{1,0:T(8,128)(2,1)}, bf16[256,512]{1,0:T(8,128)(2,1)S(1)}, u32[]{:S(2)}, u32[]{:S(2)}) collective-permute-start(bf16[256,512]{1,0:T(8,128)(2,1)} %convolution_convert_fusion.1), channel_id=1, source_target_pairs={{0,8},{2,10},{4,12},{6,14},{8,16},{10,18},{12,20},{14,22},{16,24},... | collective-permute-start | bytes 786440 | tf_op jit(solution)/shard_map/ppermute | solution.py:15
  99.5 2.8 %fusion.4 = (f32[4,4,256]{2,1,0:T(4,128)S(1)}, f32[4,256,256,4]{2,1,3,0:T(8,128)}) fusion(pred[256,256]{0,1:T(8,128)(4,1)S(1)} %get-tuple-element.28, bf16[256,4,128,1]{0,2,3,1:T(8,128)(2,1)S(1)} %bitcast.282, bf16[256,4,4,128]{3,0,2,1:T(8,128)(2,1)S(1)} %pad_maximum_fusion.1), kind=kOutput, calls=%fused_computation.15 | convolution fusion | flops 271577088 | bytes 5586944 | tf_op jit(solution)/shard_map/tkgd,skd->kgts/dot_general | solution.py:93
  102.3 0.0 collective-permute-done.4
  102.3 2.8 %fusion.3 = (f32[4,4,256]{2,1,0:T(4,128)S(1)}, f32[4,256,256,4]{2,1,3,0:T(8,128)}) fusion(pred[256,256]{0,1:T(8,128)(4,1)S(1)} %get-tuple-element.27, bf16[256,4,128,1]{0,2,3,1:T(8,128)(2,1)S(1)} %bitcast.281, bf16[256,4,4,128]{3,0,2,1:T(8,128)(2,1)S(1)} %pad_maximum_fusion.1), kind=kOutput, calls=%fused_computation.14 | convolution fusion | flops 271577088 | bytes 5586944 | tf_op jit(solution)/shard_map/tkgd,skd->kgts/dot_general | solution.py:93
  105.1 1.0 fusion.5
  106.2 2.6 %fusion.23 = f32[4,4,256,128]{2,3,1,0:T(8,128)} fusion(bf16[256,4,128,1]{0,2,3,1:T(8,128)(2,1)S(1)} %bitcast.283, f32[4,256,256,4]{2,1,3,0:T(8,128)S(1)} %get-tuple-element.41, f32[4,4,256]{2,1,0:T(4,128)S(1)} %get-tuple-element.24, pred[256,256]{0,1:T(8,128)(4,1)S(1)} %get-tuple-element.25), kind=kOutput, calls=%fused_computation.30 | convolution fusion | flops 273678336 | bytes 6635520 | tf_op jit(solution)/shard_map/kgts,skd->kgtd/dot_general | solution.py:108
  108.8 1.0 fusion.7
  109.8 0.0 collective-permute-done.1
  109.9 1.1 copy.86
  111.0 4.8 %fusion.21 = f32[4,4,256,128]{2,3,1,0:T(8,128)} fusion(bf16[256,4,128,1]{0,2,3,1:T(8,128)(2,1)S(1)} %bitcast.285, f32[4,256,256,4]{2,1,3,0:T(8,128)} %copy-done.2, f32[4,4,256]{2,1,0:T(4,128)S(1)} %get-tuple-element.17, pred[256,256]{0,1:T(8,128)(4,1)S(1)} %get-tuple-element.29), kind=kOutput, calls=%fused_computation.29 | convolution fusion | flops 273678336 | bytes 6635520 | tf_op jit(solution)/shard_map/kgts,skd->kgtd/dot_general | solution.py:108
  115.8 1.0 fusion.9
  116.8 0.0 collective-permute-done.3
  116.8 0.1 copy.89
  117.0 4.9 %fusion.19 = f32[4,4,256,128]{2,3,1,0:T(8,128)} fusion(bf16[256,4,128,1]{0,2,3,1:T(8,128)(2,1)S(1)} %bitcast.286, f32[4,256,256,4]{2,1,3,0:T(8,128)} %get-tuple-element.37, f32[4,4,256]{2,1,0:T(4,128)S(1)} %get-tuple-element.16, pred[256,256]{0,1:T(8,128)(4,1)S(1)} %get-tuple-element.26), kind=kOutput, calls=%fused_computation.28 | convolution fusion | flops 273678336 | bytes 6635520 | tf_op jit(solution)/shard_map/kgts,skd->kgtd/dot_general | solution.py:108
  121.9 1.0 fusion.11
  123.0 0.0 collective-permute-done.5
  123.0 0.1 copy.92
  123.1 4.8 %fusion.17 = f32[4,4,256,128]{2,3,1,0:T(8,128)} fusion(bf16[256,4,128,1]{0,2,3,1:T(8,128)(2,1)S(1)} %bitcast.287, f32[4,256,256,4]{2,1,3,0:T(8,128)} %get-tuple-element.35, f32[4,4,256]{2,1,0:T(4,128)S(1)} %get-tuple-element.15, pred[256,256]{0,1:T(8,128)(4,1)S(1)} %get-tuple-element.27), kind=kOutput, calls=%fused_computation.27 | convolution fusion | flops 273678336 | bytes 6635520 | tf_op jit(solution)/shard_map/kgts,skd->kgtd/dot_general | solution.py:108
  127.9 1.0 fusion.13
  129.0 0.0 collective-permute-done.7
  129.0 0.1 copy.95
  129.2 6.6 %fusion.26 = bf16[256,4,4,128]{0,3,2,1:T(8,128)(2,1)S(1)} fusion(f32[4,4,256,128]{2,3,1,0:T(8,128)} %fusion.17, f32[4,4,256,128]{2,3,1,0:T(8,128)} %fusion.19, f32[4,4,256,128]{2,3,1,0:T(8,128)} %fusion.21, f32[4,4,256,128]{2,3,1,0:T(8,128)} %fusion.23, f32[256,4,4]{0,2,1:T(4,128)S(1)} %get-tuple-element.10, f32[256,4,4]{0,2,1:T(4,128)S(1)} %get-tuple-element.13, ...), kind=kOutput, calls=%fused_computation.34 | convolution fusion | flops 279445504 | bytes 14073856 | tf_op jit(solution)/shard_map/kgts,skd->kgtd/dot_general | solution.py:108
  135.8 11.6 %convolution_convert_fusion = bf16[256,4096]{1,0:T(8,128)(2,1)} fusion(bf16[256,2048]{0,1:T(8,128)(2,1)S(1)} %bitcast.279, bf16[2048,4096]{1,0:T(8,128)(2,1)} %param.12), kind=kOutput, calls=%fused_computation | convolution fusion | flops 4296015872 | bytes 19922944 | tf_op jit(solution)/shard_map/dot_general | solution.py:129
  147.4 0.0 reduce-scatter.2.cloned.1.call-update
  147.4 19.1 %reduce-scatter.2.cloned.1.call-done = bf16[128,4096]{1,0:T(8,128)(2,1)} async-done(((bf16[256,4096]{1,0:T(8,128)(2,1)}), bf16[128,4096]{1,0:T(8,128)(2,1)}) %reduce-scatter.2.cloned.1.call-update) | async-done | bytes 1048592 | tf_op jit(solution)/shard_map/reduce_scatter | solution.py:128
  (34 shorter events, 0.1 us)
Async XLA Ops:
  9.6 13.7 %all-to-all-start = ((bf16[2,128,4096]{2,1,0:T(8,128)(2,1)}), bf16[2,128,4096]{2,1,0:T(8,128)(2,1)S(1)}, u32[]{:S(2)}, u32[]{:S(2)}) async-start(bf16[2,128,4096]{2,1,0:T(8,128)(2,1)} %pad_maximum_fusion), calls=%async_computation | async-start | bytes 4194304 | tf_op jit(solution)/shard_map/all_to_all | solution.py:53
  16.6 149.9 %reduce-scatter.2.cloned.1.call-start = ((), (), s32[]{:S(2)}) async-start(), calls=%async_computation.2 | async-start | bytes 3145728 | tf_op jit(solution)/shard_map/reduce_scatter | solution.py:128
  16.6 6.4 %copy-start.13 = (f32[64]{0:T(128)S(1)}, f32[64]{0:T(128)}, u32[]{:S(2)}) copy-start(f32[64]{0:T(128)} %constant.39.clone) | copy-start | bytes 772
  23.3 17.6 %copy-start.14 = (bf16[4096,512]{1,0:T(8,128)(2,1)S(1)}, bf16[4096,512]{1,0:T(8,128)(2,1)}, u32[]{:S(2)}) copy-start(bf16[4096,512]{1,0:T(8,128)(2,1)} %param.11) | copy-start | bytes 12582916
  27.8 22.2 %copy-start.7 = (s32[64]{0:T(128)S(1)}, s32[64]{0:T(128)}, u32[]{:S(2)}) copy-start(s32[64]{0:T(128)} %param.8) | copy-start | bytes 772
  27.8 55.8 %collective-permute-start = (bf16[256,512]{0,1:T(8,128)(2,1)}, bf16[256,512]{0,1:T(8,128)(2,1)}, u32[]{:S(2)}, u32[]{:S(2)}) collective-permute-start(bf16[256,512]{0,1:T(8,128)(2,1)} %bitcast.18), channel_id=1, source_target_pairs={{0,2},{2,4},{4,6},{6,8},{8,10},{10,12},{12,14},{14,16},{16,18},{18... | collective-permute-start | bytes 786440 | tf_op jit(solution)/shard_map/ppermute | solution.py:15
  30.0 57.9 %collective-permute-start.2 = (bf16[256,512]{0,1:T(8,128)(2,1)}, bf16[256,512]{0,1:T(8,128)(2,1)}, u32[]{:S(2)}, u32[]{:S(2)}) collective-permute-start(bf16[256,512]{0,1:T(8,128)(2,1)} %bitcast.18), channel_id=1, source_target_pairs={{0,4},{2,6},{4,8},{6,10},{8,12},{10,14},{12,16},{14,18},{16,20},{1... | collective-permute-start | bytes 786440 | tf_op jit(solution)/shard_map/ppermute | solution.py:15
  34.4 61.7 %collective-permute-start.6 = (bf16[256,512]{0,1:T(8,128)(2,1)}, bf16[256,512]{0,1:T(8,128)(2,1)S(1)}, u32[]{:S(2)}, u32[]{:S(2)}) collective-permute-start(bf16[256,512]{0,1:T(8,128)(2,1)} %bitcast.18), channel_id=1, source_target_pairs={{0,8},{2,10},{4,12},{6,14},{8,16},{10,18},{12,20},{14,22},{16,24},... | collective-permute-start | bytes 786440 | tf_op jit(solution)/shard_map/ppermute | solution.py:15
  36.9 65.4 %collective-permute-start.4 = (bf16[256,512]{0,1:T(8,128)(2,1)}, bf16[256,512]{0,1:T(8,128)(2,1)S(1)}, u32[]{:S(2)}, u32[]{:S(2)}) collective-permute-start(bf16[256,512]{0,1:T(8,128)(2,1)} %bitcast.18), channel_id=1, source_target_pairs={{0,6},{2,8},{4,10},{6,12},{8,14},{10,16},{12,18},{14,20},{16,22},{... | collective-permute-start | bytes 786440 | tf_op jit(solution)/shard_map/ppermute | solution.py:15
  43.0 66.8 %collective-permute-start.1 = (bf16[256,512]{1,0:T(8,128)(2,1)}, bf16[256,512]{1,0:T(8,128)(2,1)}, u32[]{:S(2)}, u32[]{:S(2)}) collective-permute-start(bf16[256,512]{1,0:T(8,128)(2,1)} %convolution_convert_fusion.1), channel_id=1, source_target_pairs={{0,2},{2,4},{4,6},{6,8},{8,10},{10,12},{12,14},{14,16},{16,18},{18... | collective-permute-start | bytes 786440 | tf_op jit(solution)/shard_map/ppermute | solution.py:15
  80.1 1.6 copy-start.5
  80.1 1.6 copy-start.6
  80.1 1.8 %copy-start.8 = (pred[256]{0:T(512)(128)(4,1)S(1)}, pred[256]{0:T(512)(128)(4,1)}, u32[]{:S(2)}) copy-start(pred[256]{0:T(512)(128)(4,1)} %get-tuple-element.48) | copy-start | bytes 772
  80.1 1.7 %copy-start.9 = (pred[256]{0:T(512)(128)(4,1)S(1)}, pred[256]{0:T(512)(128)(4,1)}, u32[]{:S(2)}) copy-start(pred[256]{0:T(512)(128)(4,1)} %get-tuple-element.49) | copy-start | bytes 772
  80.1 1.7 %copy-start.10 = (pred[256]{0:T(512)(128)(4,1)S(1)}, pred[256]{0:T(512)(128)(4,1)}, u32[]{:S(2)}) copy-start(pred[256]{0:T(512)(128)(4,1)} %get-tuple-element.50) | copy-start | bytes 772
  80.1 1.7 %copy-start.11 = (pred[256]{0:T(512)(128)(4,1)S(1)}, pred[256]{0:T(512)(128)(4,1)}, u32[]{:S(2)}) copy-start(pred[256]{0:T(512)(128)(4,1)} %get-tuple-element.51) | copy-start | bytes 772
  80.1 1.7 %copy-start.12 = (pred[256]{0:T(512)(128)(4,1)S(1)}, pred[256]{0:T(512)(128)(4,1)}, u32[]{:S(2)}) copy-start(pred[256]{0:T(512)(128)(4,1)} %broadcast_compare_fusion.3) | copy-start | bytes 772
  83.6 33.3 %collective-permute-start.3 = (bf16[256,512]{1,0:T(8,128)(2,1)}, bf16[256,512]{1,0:T(8,128)(2,1)S(1)}, u32[]{:S(2)}, u32[]{:S(2)}) collective-permute-start(bf16[256,512]{1,0:T(8,128)(2,1)} %convolution_convert_fusion.1), channel_id=1, source_target_pairs={{0,4},{2,6},{4,8},{6,10},{8,12},{10,14},{12,16},{14,18},{16,20},{1... | collective-permute-start | bytes 786440 | tf_op jit(solution)/shard_map/ppermute | solution.py:15
  87.9 20.9 %copy-start.2 = (f32[4,256,256,4]{2,1,3,0:T(8,128)}, f32[4,256,256,4]{2,1,3,0:T(8,128)S(1)}, u32[]{:S(2)}) copy-start(f32[4,256,256,4]{2,1,3,0:T(8,128)S(1)} %get-tuple-element.39) | copy-start | bytes 12582916
  87.9 35.1 %collective-permute-start.5 = (bf16[256,512]{1,0:T(8,128)(2,1)}, bf16[256,512]{1,0:T(8,128)(2,1)S(1)}, u32[]{:S(2)}, u32[]{:S(2)}) collective-permute-start(bf16[256,512]{1,0:T(8,128)(2,1)} %convolution_convert_fusion.1), channel_id=1, source_target_pairs={{0,6},{2,8},{4,10},{6,12},{8,14},{10,16},{12,18},{14,20},{16,22},{... | collective-permute-start | bytes 786440 | tf_op jit(solution)/shard_map/ppermute | solution.py:15
  96.1 32.9 %collective-permute-start.7 = (bf16[256,512]{1,0:T(8,128)(2,1)}, bf16[256,512]{1,0:T(8,128)(2,1)S(1)}, u32[]{:S(2)}, u32[]{:S(2)}) collective-permute-start(bf16[256,512]{1,0:T(8,128)(2,1)} %convolution_convert_fusion.1), channel_id=1, source_target_pairs={{0,8},{2,10},{4,12},{6,14},{8,16},{10,18},{12,20},{14,22},{16,24},... | collective-permute-start | bytes 786440 | tf_op jit(solution)/shard_map/ppermute | solution.py:15
  102.3 3.9 %copy-start.4 = (bf16[256,512]{0,1:T(8,128)(2,1)S(1)}, bf16[256,512]{0,1:T(8,128)(2,1)}, u32[]{:S(2)}) copy-start(bf16[256,512]{0,1:T(8,128)(2,1)} %copy.83) | copy-start | bytes 786436
  110.9 4.8 %copy-start.1 = (f32[4,256,256,4]{2,1,3,0:T(8,128)S(1)}, f32[4,256,256,4]{2,1,3,0:T(8,128)}, u32[]{:S(2)}) copy-start(f32[4,256,256,4]{2,1,3,0:T(8,128)} %get-tuple-element.37) | copy-start | bytes 12582916
  117.0 4.9 %copy-start.3 = (f32[4,256,256,4]{2,1,3,0:T(8,128)S(1)}, f32[4,256,256,4]{2,1,3,0:T(8,128)}, u32[]{:S(2)}) copy-start(f32[4,256,256,4]{2,1,3,0:T(8,128)} %get-tuple-element.35) | copy-start | bytes 12582916
  123.1 4.8 %copy-start = (f32[4,256,256,4]{2,1,3,0:T(8,128)S(1)}, f32[4,256,256,4]{2,1,3,0:T(8,128)}, u32[]{:S(2)}) copy-start(f32[4,256,256,4]{2,1,3,0:T(8,128)} %get-tuple-element.33) | copy-start | bytes 12582916
Sparse Core Ops, SparseCore 0:
  147.5 18.9 reduce-scatter.1
